TPU v7x, 256 devices: a whole 4x4x8 slice. The times are simulated.
256 devices in a mesh: brick: 8 (over x_lo, y), bulk: 32 (over x_hi, z, core).
Axes of the slice: x: 4 (x_hi: 2, x_lo: 2; x = x_hi * 2 + x_lo), y: 4, z: 8, core: 2. Of those that a mesh axis runs over, the one named last changes fastest.
Arguments:
- amp_traces: float32 [128, 2048, 256], P(None, ('bulk', 'brick')), may hold values from -6 to 6
- patch_owner: int32 [524288, 1], P(('brick', 'bulk')), may hold values from 0 to 31; in each aligned block of 2048 rows (0 to 2047, 2048 to 4095, ...) at most 256 rows name the same one
- patch_fault: int32 [524288], P(('brick', 'bulk')), may hold values from 0 to 15
- patch_trace: int32 [524288], P(('brick', 'bulk')), may hold values from 0 to 1023
- patch_offset: int32 [524288], P(('brick', 'bulk')), may hold values from 0 to 128
Outputs:
- fault_attr: float32 [128, 2048, 256], P('brick', 'bulk')
- fault_profile: float32 [4096, 128], P(('brick', 'bulk'))
Inputs may be any that keep to these rules, and one draw needn't show every extreme that they name: `patch_owner`: among the 2048 patches of one device, at most 256 name the same owner, and in every draw some device has exactly 256 patches with one owner.
All inputs are finite; a program needn't handle non-finite values.
Results may differ from a plain program's by a relative error of at most 0.0003.
Values sent between devices are 32-bit elements; how exact they have to be, the bound alone decides.
A program may use at most 64 MiB of HBM per device.

v0:
```python
import jax
import jax.numpy as jnp
from jax import lax
from jax.sharding import PartitionSpec as P

PATCH = 128
F_DEV = 16


def padded_2(block, sides, width):
    for axis, dim in sides:
        count = lax.axis_size(axis)
        forward = [(i, i + 1) for i in range(count - 1)]
        backward = [(target, source) for source, target in forward]
        low = lax.ppermute(
            lax.slice_in_dim(block, block.shape[dim] - width, None, axis=dim), axis, forward
        )
        high = lax.ppermute(lax.slice_in_dim(block, 0, width, axis=dim), axis, backward)
        block = jnp.concatenate([low, block, high], axis=dim)
    return block


def box_sum(values, radius, dimension):
    length = values.shape[dimension] - 2 * radius
    summed = lax.slice_in_dim(values, 0, length, axis=dimension)
    for offset in range(1, 2 * radius + 1):
        summed = summed + lax.slice_in_dim(values, offset, offset + length, axis=dimension)
    return summed


def time_sum(values, radius):
    widths = [(0, 0)] * (values.ndim - 1) + [(radius, radius)]
    return box_sum(jnp.pad(values, widths), radius, values.ndim - 1)


def gradient_energy(padded):
    slope_inline = 0.5 * (padded[2:, 1:-1, :] - padded[:-2, 1:-1, :])
    slope_cross = 0.5 * (padded[1:-1, 2:, :] - padded[1:-1, :-2, :])
    centre = jnp.pad(padded[1:-1, 1:-1, :], ((0, 0), (0, 0), (1, 1)))
    slope_time = 0.5 * (centre[:, :, 2:] - centre[:, :, :-2])
    return jnp.stack(
        [slope_inline * slope_inline, slope_cross * slope_cross, slope_time * slope_time]
    )


def smooth_tensor(energy):
    return time_sum(box_sum(box_sum(energy, 2, 1), 2, 2), 2)


def finish(tensor, near_amp):
    lateral = (tensor[0] + tensor[1]) / (tensor[0] + tensor[1] + tensor[2] + 1e-05)
    stack = box_sum(box_sum(near_amp, 1, 0), 1, 1)
    power = box_sum(box_sum(near_amp * near_amp, 1, 0), 1, 1)
    semblance = time_sum(stack * stack, 4) / (9.0 * time_sum(power, 4) + 1e-05)
    return (1.0 - semblance) * lateral


def window_rows(chosen, offsets, width):
    samples = chosen.shape[1]
    steps = (samples - width).bit_length()
    current = chosen
    for level in range(steps):
        amount = 1 << level
        moved = jnp.concatenate(
            [current[:, amount:], jnp.zeros((current.shape[0], amount), current.dtype)], axis=1
        )
        taken = (offsets >> level & 1)[:, None] == 1
        current = jnp.where(taken, moved, current)
    return current[:, :width]


def local(amp_traces, patch_owner, patch_fault, patch_trace, patch_offset):
    bricked = lax.all_to_all(amp_traces, "brick", split_axis=0, concat_axis=1, tiled=True)
    near_amp = padded_2(bricked, (("brick", 0), ("bulk", 1)), 1)
    energy = gradient_energy(near_amp)
    rimmed = padded_2(energy, (("brick", 1), ("bulk", 2)), 2)
    attribute = finish(smooth_tensor(rimmed), near_amp)
    flattened = attribute.reshape(-1, attribute.shape[2])
    chosen = flattened[patch_trace]
    patch_rows = window_rows(chosen, patch_offset, PATCH)
    owners = patch_owner[:, 0]
    owner_count = lax.axis_size("bulk")
    count_patches = patch_rows.shape[0]
    one_hot = (owners[:, None] == jnp.arange(owner_count, dtype=jnp.int32)[None, :]).astype(
        jnp.int32
    )
    placed = jnp.cumsum(one_hot, axis=0)
    slot_rank = jnp.sum(placed * one_hot, axis=1) - 1
    capacity = 4 * count_patches // owner_count
    buffer = (
        jnp.zeros((owner_count, capacity, PATCH), jnp.float32).at[owners, slot_rank].set(patch_rows)
    )
    labels = (
        jnp.zeros((owner_count, capacity), jnp.float32)
        .at[owners, slot_rank]
        .set(patch_fault.astype(jnp.float32) + 1.0)
    )
    got_rows, got_labels = (
        lax.all_to_all(buffer, "bulk", split_axis=0, concat_axis=0, tiled=True),
        lax.all_to_all(labels, "bulk", split_axis=0, concat_axis=0, tiled=True),
    )
    wanted = jnp.arange(F_DEV, dtype=jnp.float32) + 1.0
    selector = (got_labels.reshape(1, -1) == wanted[:, None]).astype(jnp.float32)
    summed = jnp.dot(
        selector,
        got_rows.reshape(-1, PATCH),
        precision=lax.Precision.HIGHEST,
        preferred_element_type=jnp.float32,
    )
    counts = jnp.sum(selector, axis=1)
    profile = summed / jnp.maximum(counts, 1.0)[:, None]
    return (attribute, profile)


def solution(mesh):
    in_specs = (
        P(None, ("bulk", "brick"), None),
        P(("brick", "bulk"), None),
        P(("brick", "bulk")),
        P(("brick", "bulk")),
        P(("brick", "bulk")),
    )
    out_specs = (P("brick", "bulk", None), P(("brick", "bulk"), None))
    return jax.shard_map(local, mesh=mesh, in_specs=in_specs, out_specs=out_specs, check_vma=False)
```

profile of v0, /device:TPU:24, one launch (start us, length us, event | category | flops | bytes accessed | tf_op | source)
XLA Modules:
  0.0 232.0 jit_solution(7785057367832346467)
XLA Ops:
  0.6 0.0 copy-start.6
  0.6 0.0 copy-start.5
  0.7 5.8 %all-to-all-start = ((f32[128,8,256]{2,1,0:T(8,128)}), f32[128,8,256]{2,1,0:T(8,128)S(1)}, u32[]{:S(2)}, u32[]{:S(2)}) async-start(f32[128,8,256]{2,1,0:T(8,128)} %param.5), calls=%async_computation | async-start | bytes 2097152 | tf_op jit(solution)/shard_map/all_to_all | solution.py:73
  6.5 9.1 %reduce-window.6 = s32[32,16,128]{2,1,0:T(8,128)S(1)} reduce-window(s32[32,16,128]{2,1,0:T(8,128)S(1)} %fusion.51, s32[]{:T(128)} %constant.22.clone.1), window={size=1x1x128 pad=0_0x0_0x127_0}, to_apply=%region_0.1 | reduce-window | flops 8323072 | bytes 524292 | tf_op jit(solution)/shard_map/reduce-window
  15.5 0.1 slice.326
  15.7 0.2 copy.14
  15.9 0.2 reduce-window.9
  16.1 0.1 broadcast_add_fusion
  16.3 0.0 copy-start.4
  16.3 0.1 fusion.48
  16.4 0.1 multiply_reduce_fusion
  16.5 0.1 and_reduce_fusion
  16.7 8.6 %scatter_custom_fusion = f32[8192]{0:T(1024)} fusion(s32[2048]{0:T(1024)S(1)} %broadcast_select_fusion, f32[2048]{0:T(1024)S(1)} %convert_add_fusion, f32[]{:T(128)} %constant.18.clone.1), kind=kCustom, calls=%fused_computation.139 | custom fusion | bytes 32772
  25.3 0.0 all-to-all-done
  25.3 11.0 %all-to-all-start.1 = ((f32[32,1,256]{2,1,0:T(1,128)}), f32[32,1,256]{2,1,0:T(1,128)S(1)}, u32[]{:S(2)}, u32[]{:S(2)}) async-start(f32[32,1,256]{2,1,0:T(1,128)} %bitcast.18), calls=%async_computation.1 | async-start | bytes 65536 | tf_op jit(solution)/shard_map/all_to_all | solution.py:100
  36.3 0.1 copy.19
  36.5 2.8 %collective-permute-start = (f32[1,64,256]{2,1,0:T(8,128)S(1)}, f32[1,64,256]{2,1,0:T(8,128)S(1)}, u32[]{:S(2)}, u32[]{:S(2)}) collective-permute-start(f32[1,64,256]{2,1,0:T(8,128)S(1)} %get-tuple-element.13), channel_id=1, source_target_pairs={{0,32},{32,64},{64,96},{96,128},{128,160},{160,192},{192,224},{1,3... | collective-permute-start | bytes 196616 | tf_op jit(solution)/shard_map/ppermute | solution.py:15
  39.2 3.1 %collective-permute-start.1 = (f32[1,64,256]{2,1,0:T(8,128)S(1)}, f32[1,64,256]{2,1,0:T(8,128)S(1)}, u32[]{:S(2)}, u32[]{:S(2)}) collective-permute-start(f32[1,64,256]{2,1,0:T(8,128)S(1)} %get-tuple-element.14), channel_id=1, source_target_pairs={{32,0},{64,32},{96,64},{128,96},{160,128},{192,160},{224,192},{33,... | collective-permute-start | bytes 196616 | tf_op jit(solution)/shard_map/ppermute | solution.py:18
  42.3 0.3 collective-permute-done
  42.6 4.9 %collective-permute-done.1 = f32[1,64,256]{2,1,0:T(8,128)S(1)} collective-permute-done((f32[1,64,256]{2,1,0:T(8,128)S(1)}, f32[1,64,256]{2,1,0:T(8,128)S(1)}, u32[]{:S(2)}, u32[]{:S(2)}) %collective-permute-start.1) | collective-permute-done | bytes 65568 | tf_op jit(solution)/shard_map/ppermute | solution.py:18
  47.5 1.3 collective-permute-start.2
  48.8 1.3 collective-permute-start.3
  50.2 3.8 %collective-permute-done.3 = f32[18,1,256]{2,1,0:T(1,128)S(1)} collective-permute-done((f32[18,1,256]{2,1,0:T(1,128)S(1)}, f32[18,1,256]{2,1,0:T(1,128)S(1)}, u32[]{:S(2)}, u32[]{:S(2)}) %collective-permute-start.3) | collective-permute-done | bytes 18464 | tf_op jit(solution)/shard_map/ppermute | solution.py:18
  53.9 0.9 fusion.42
  54.9 0.1 pad_maximum_fusion.12
  54.9 1.9 collective-permute-start.4
  56.8 3.9 %collective-permute-start.5 = (f32[3,2,64,256]{3,2,1,0:T(8,128)S(1)}, f32[3,2,64,256]{3,2,1,0:T(8,128)S(1)}, u32[]{:S(2)}, u32[]{:S(2)}) collective-permute-start(f32[3,2,64,256]{3,2,1,0:T(8,128)S(1)} %get-tuple-element.5), channel_id=1, source_target_pairs={{32,0},{64,32},{96,64},{128,96},{160,128},{192,160},{224,192},{33,... | collective-permute-start | bytes 1179656 | tf_op jit(solution)/shard_map/ppermute | solution.py:18
  60.8 0.2 pad_maximum_fusion.1
  61.0 0.2 slice_add_fusion.8
  61.2 0.2 fusion.43
  61.4 5.9 %collective-permute-done.4 = f32[3,2,64,256]{3,2,1,0:T(8,128)S(1)} collective-permute-done((f32[3,2,64,256]{3,2,1,0:T(8,128)S(1)}, f32[3,2,64,256]{3,2,1,0:T(8,128)S(1)}, u32[]{:S(2)}, u32[]{:S(2)}) %collective-permute-start.4) | collective-permute-done | bytes 393248 | tf_op jit(solution)/shard_map/ppermute | solution.py:15
  67.3 4.0 %collective-permute-done.5 = f32[3,2,64,256]{3,2,1,0:T(8,128)S(1)} collective-permute-done((f32[3,2,64,256]{3,2,1,0:T(8,128)S(1)}, f32[3,2,64,256]{3,2,1,0:T(8,128)S(1)}, u32[]{:S(2)}, u32[]{:S(2)}) %collective-permute-start.5) | collective-permute-done | bytes 393248 | tf_op jit(solution)/shard_map/ppermute | solution.py:18
  71.3 0.1 pad_maximum_fusion.17
  71.4 3.3 %collective-permute-start.6 = (f32[3,20,2,256]{3,2,1,0:T(2,128)S(1)}, f32[3,20,2,256]{3,2,1,0:T(2,128)S(1)}, u32[]{:S(2)}, u32[]{:S(2)}) collective-permute-start(f32[3,20,2,256]{3,2,1,0:T(2,128)S(1)} %get-tuple-element.2), channel_id=1, source_target_pairs={{0,1},{1,2},{2,3},{3,4},{4,5},{5,6},{6,7},{7,8},{8,9},{9,10},{10,1... | collective-permute-start | bytes 368648 | tf_op jit(solution)/shard_map/ppermute | solution.py:15
  74.7 1.5 collective-permute-start.7
  76.1 0.2 slice_add_fusion.13
  76.4 3.1 %collective-permute-done.7 = f32[3,20,2,256]{3,2,1,0:T(2,128)S(1)} collective-permute-done((f32[3,20,2,256]{3,2,1,0:T(2,128)S(1)}, f32[3,20,2,256]{3,2,1,0:T(2,128)S(1)}, u32[]{:S(2)}, u32[]{:S(2)}) %collective-permute-start.7) | collective-permute-done | bytes 122912 | tf_op jit(solution)/shard_map/ppermute | solution.py:18
  79.5 0.9 pad_maximum_fusion
  80.4 0.5 slice_add_fusion
  80.9 1.2 slice_add_fusion.4
  82.1 4.9 %fusion.3 = f32[3,16,64,256]{3,2,1,0:T(8,128)} fusion(f32[3,16,64,256]{3,2,1,0:T(8,128)S(1)} %slice_add_fusion.4), kind=kLoop, calls=%fused_computation.15 | loop fusion | flops 3145728 | bytes 6291456 | tf_op jit(solution)/shard_map/add | solution.py:27
  87.1 5.9 %fusion.33 = f32[16,64,256]{2,1,0:T(8,128)S(1)} fusion(f32[3,16,64,256]{3,2,1,0:T(8,128)} %fusion.3, f32[16,64,256]{2,1,0:T(8,128)S(1)} %slice_add_fusion.13, f32[16,64,256]{2,1,0:T(8,128)S(1)} %fusion.43), kind=kLoop, calls=%fused_computation.82 | loop fusion | flops 6553600 | bytes 6291456 | tf_op jit(solution)/shard_map/mul | solution.py:55
  92.9 0.0 copy-start
  92.9 6.6 %gather_fusion = f32[2048,256]{1,0:T(8,128)S(1)} fusion(f32[1024,256]{1,0:T(8,128)S(1)} %bitcast.57, s32[2048]{0:T(1024)S(1)} %fusion.54), kind=kCustom, calls=%fused_computation | custom fusion | bytes 4202496 | tf_op jit(solution)/shard_map/gather | solution.py:79
  99.6 0.6 slice.328
  100.2 0.5 pad_select_fusion.6
  100.7 0.6 slice.329
  101.3 0.4 pad_select_fusion.5
  101.8 0.6 slice.330
  102.4 0.4 pad_select_fusion.4
  102.8 0.6 slice.331
  103.4 0.4 pad_select_fusion.3
  103.9 0.6 slice.332
  104.5 0.7 pad_select_fusion.2
  105.2 0.6 slice.333
  105.8 0.4 pad_select_fusion.1
  106.2 0.6 slice.334
  106.8 0.4 pad_select_fusion
  107.3 0.1 slice.335
  107.4 8.9 %scatter_custom_fusion.1 = f32[8192,128]{1,0:T(8,128)} fusion(s32[2048]{0:T(1024)S(1)} %broadcast_select_fusion, f32[]{:T(128)} %constant.18.clone.1, f32[2048,256]{1,0:T(8,128)S(1)} %pad_select_fusion, f32[2048,128]{1,0:T(8,128)S(1)} %slice.335, pred[2048]{0:T(1024)(128)(4,1)S(1)} %get-tuple-element.17), kind=kCustom, calls=%fused_computation.36 | custom fusion | flops 262144 | bytes 6294528
  116.3 14.7 %all-to-all-start.2 = ((f32[32,256,128]{2,1,0:T(8,128)}), f32[32,256,128]{2,1,0:T(8,128)}, u32[]{:S(2)}, u32[]{:S(2)}) async-start(f32[32,256,128]{2,1,0:T(8,128)} %bitcast.62), calls=%async_computation.2 | async-start | bytes 8388608 | tf_op jit(solution)/shard_map/all_to_all | solution.py:99
  131.0 0.3 fusion.45
  131.3 96.4 %all-to-all-done.2 = f32[32,256,128]{2,1,0:T(8,128)} async-done(((f32[32,256,128]{2,1,0:T(8,128)}), f32[32,256,128]{2,1,0:T(8,128)}, u32[]{:S(2)}, u32[]{:S(2)}) %all-to-all-start.2) | async-done | bytes 4194336 | tf_op jit(solution)/shard_map/all_to_all | solution.py:99
  227.7 4.3 %convolution_divide_fusion = f32[16,128]{1,0:T(8,128)} fusion(f32[8192,128]{1,0:T(8,128)} %bitcast.22, f32[8192]{0:T(1024)S(1)} %bitcast.66, f32[16]{0:T(128)S(1)} %iota_add_fusion, f32[16]{0:T(128)S(1)} %broadcast_maximum_fusion), kind=kOutput, calls=%fused_computation.52 | convolution fusion | flops 201459712 | bytes 4235392 | tf_op jit(solution)/shard_map/dot_general | solution.py:104
  (24 shorter events, 0.2 us)
Async XLA Ops:
  0.6 15.8 %copy-start.6 = (s32[2]{0:T(128)S(1)}, s32[2]{0:T(128)}, u32[]{:S(2)}) copy-start(s32[2]{0:T(128)} %constant.79) | copy-start | bytes 28
  0.6 15.9 %copy-start.5 = (s32[2]{0:T(128)S(1)}, s32[2]{0:T(128)}, u32[]{:S(2)}) copy-start(s32[2]{0:T(128)} %constant.82) | copy-start | bytes 28
  0.7 5.8 %copy-start.1 = (s32[2048,1]{0,1:T(1,128)S(1)}, s32[2048,1]{0,1:T(1,128)}, u32[]{:S(2)}) copy-start(s32[2048,1]{0,1:T(1,128)} %param.6) | copy-start | bytes 24580
  0.7 16.0 %copy-start.3 = (s32[2048]{0:T(1024)S(1)}, s32[2048]{0:T(1024)}, u32[]{:S(2)}) copy-start(s32[2048]{0:T(1024)} %param.7) | copy-start | bytes 24580
  0.7 24.6 %all-to-all-start = ((f32[128,8,256]{2,1,0:T(8,128)}), f32[128,8,256]{2,1,0:T(8,128)S(1)}, u32[]{:S(2)}, u32[]{:S(2)}) async-start(f32[128,8,256]{2,1,0:T(8,128)} %param.5), calls=%async_computation | async-start | bytes 2097152 | tf_op jit(solution)/shard_map/all_to_all | solution.py:73
  15.5 26.8 %copy-start.2 = (s32[2048]{0:T(1024)S(1)}, s32[2048]{0:T(1024)}, u32[]{:S(2)}) copy-start(s32[2048]{0:T(1024)} %param.9) | copy-start | bytes 24580
  16.3 33.9 %copy-start.4 = (s32[2048]{0:T(1024)S(1)}, s32[2048]{0:T(1024)}, u32[]{:S(2)}) copy-start(s32[2048]{0:T(1024)} %param.8) | copy-start | bytes 24580
  25.3 91.0 %all-to-all-start.1 = ((f32[32,1,256]{2,1,0:T(1,128)}), f32[32,1,256]{2,1,0:T(1,128)S(1)}, u32[]{:S(2)}, u32[]{:S(2)}) async-start(f32[32,1,256]{2,1,0:T(1,128)} %bitcast.18), calls=%async_computation.1 | async-start | bytes 65536 | tf_op jit(solution)/shard_map/all_to_all | solution.py:100
  36.5 6.2 %collective-permute-start = (f32[1,64,256]{2,1,0:T(8,128)S(1)}, f32[1,64,256]{2,1,0:T(8,128)S(1)}, u32[]{:S(2)}, u32[]{:S(2)}) collective-permute-start(f32[1,64,256]{2,1,0:T(8,128)S(1)} %get-tuple-element.13), channel_id=1, source_target_pairs={{0,32},{32,64},{64,96},{96,128},{128,160},{160,192},{192,224},{1,3... | collective-permute-start | bytes 196616 | tf_op jit(solution)/shard_map/ppermute | solution.py:15
  39.2 8.3 %collective-permute-start.1 = (f32[1,64,256]{2,1,0:T(8,128)S(1)}, f32[1,64,256]{2,1,0:T(8,128)S(1)}, u32[]{:S(2)}, u32[]{:S(2)}) collective-permute-start(f32[1,64,256]{2,1,0:T(8,128)S(1)} %get-tuple-element.14), channel_id=1, source_target_pairs={{32,0},{64,32},{96,64},{128,96},{160,128},{192,160},{224,192},{33,... | collective-permute-start | bytes 196616 | tf_op jit(solution)/shard_map/ppermute | solution.py:18
  47.5 2.6 %collective-permute-start.2 = (f32[18,1,256]{2,1,0:T(1,128)S(1)}, f32[18,1,256]{2,1,0:T(1,128)S(1)}, u32[]{:S(2)}, u32[]{:S(2)}) collective-permute-start(f32[18,1,256]{2,1,0:T(1,128)S(1)} %get-tuple-element.11), channel_id=1, source_target_pairs={{0,1},{1,2},{2,3},{3,4},{4,5},{5,6},{6,7},{7,8},{8,9},{9,10},{10,1... | collective-permute-start | bytes 55304 | tf_op jit(solution)/shard_map/ppermute | solution.py:15
  48.8 5.1 %collective-permute-start.3 = (f32[18,1,256]{2,1,0:T(1,128)S(1)}, f32[18,1,256]{2,1,0:T(1,128)S(1)}, u32[]{:S(2)}, u32[]{:S(2)}) collective-permute-start(f32[18,1,256]{2,1,0:T(1,128)S(1)} %get-tuple-element.10), channel_id=1, source_target_pairs={{1,0},{2,1},{3,2},{4,3},{5,4},{6,5},{7,6},{8,7},{9,8},{10,9},{11,1... | collective-permute-start | bytes 55304 | tf_op jit(solution)/shard_map/ppermute | solution.py:18
  54.9 12.4 %collective-permute-start.4 = (f32[3,2,64,256]{3,2,1,0:T(8,128)S(1)}, f32[3,2,64,256]{3,2,1,0:T(8,128)S(1)}, u32[]{:S(2)}, u32[]{:S(2)}) collective-permute-start(f32[3,2,64,256]{3,2,1,0:T(8,128)S(1)} %get-tuple-element.4), channel_id=1, source_target_pairs={{0,32},{32,64},{64,96},{96,128},{128,160},{160,192},{192,224},{1,3... | collective-permute-start | bytes 1179656 | tf_op jit(solution)/shard_map/ppermute | solution.py:15
  56.8 14.5 %collective-permute-start.5 = (f32[3,2,64,256]{3,2,1,0:T(8,128)S(1)}, f32[3,2,64,256]{3,2,1,0:T(8,128)S(1)}, u32[]{:S(2)}, u32[]{:S(2)}) collective-permute-start(f32[3,2,64,256]{3,2,1,0:T(8,128)S(1)} %get-tuple-element.5), channel_id=1, source_target_pairs={{32,0},{64,32},{96,64},{128,96},{160,128},{192,160},{224,192},{33,... | collective-permute-start | bytes 1179656 | tf_op jit(solution)/shard_map/ppermute | solution.py:18
  71.4 5.0 %collective-permute-start.6 = (f32[3,20,2,256]{3,2,1,0:T(2,128)S(1)}, f32[3,20,2,256]{3,2,1,0:T(2,128)S(1)}, u32[]{:S(2)}, u32[]{:S(2)}) collective-permute-start(f32[3,20,2,256]{3,2,1,0:T(2,128)S(1)} %get-tuple-element.2), channel_id=1, source_target_pairs={{0,1},{1,2},{2,3},{3,4},{4,5},{5,6},{6,7},{7,8},{8,9},{9,10},{10,1... | collective-permute-start | bytes 368648 | tf_op jit(solution)/shard_map/ppermute | solution.py:15
  74.7 4.8 %collective-permute-start.7 = (f32[3,20,2,256]{3,2,1,0:T(2,128)S(1)}, f32[3,20,2,256]{3,2,1,0:T(2,128)S(1)}, u32[]{:S(2)}, u32[]{:S(2)}) collective-permute-start(f32[3,20,2,256]{3,2,1,0:T(2,128)S(1)} %get-tuple-element.3), channel_id=1, source_target_pairs={{1,0},{2,1},{3,2},{4,3},{5,4},{6,5},{7,6},{8,7},{9,8},{10,9},{11,1... | collective-permute-start | bytes 368648 | tf_op jit(solution)/shard_map/ppermute | solution.py:18
  92.9 6.7 %copy-start = (f32[16,64,256]{2,1,0:T(8,128)}, f32[16,64,256]{2,1,0:T(8,128)S(1)}, u32[]{:S(2)}) copy-start(f32[16,64,256]{2,1,0:T(8,128)S(1)} %fusion.33) | copy-start | bytes 3145732
  116.3 111.4 %all-to-all-start.2 = ((f32[32,256,128]{2,1,0:T(8,128)}), f32[32,256,128]{2,1,0:T(8,128)}, u32[]{:S(2)}, u32[]{:S(2)}) async-start(f32[32,256,128]{2,1,0:T(8,128)} %bitcast.62), calls=%async_computation.2 | async-start | bytes 8388608 | tf_op jit(solution)/shard_map/all_to_all | solution.py:99
where the time goes:
time: 232 us
  waiting for transfers between devices  118 us (51%)
  starting transfers between devices  50.5 us (22%)
  other arithmetic  37.7 us (16%)
  local copies, waits for them, and re-layouts  20.1 us (9%)
  matrix products  4.29 us (2%)
    all_to_all x1, waiting for transfers between devices, local(): lax.all_to_all(buffer, 'bulk', split_axis=0, concat_axis=0, tiled=True)  96.4 us
    ppermute x4, waiting for transfers between devices, padded_2(): lax.ppermute(lax.slice_in_dim(block, 0, width, axis=dim), axis, backward)  15.8 us
    all_to_all x1, starting transfers between devices, local(): lax.all_to_all(buffer, 'bulk', split_axis=0, concat_axis=0, tiled=True)  14.7 us
    all_to_all x1, starting transfers between devices, local(): lax.all_to_all(labels, 'bulk', split_axis=0, concat_axis=0, tiled=True)  11 us
    ppermute x4, starting transfers between devices, padded_2(): lax.ppermute(lax.slice_in_dim(block, 0, width, axis=dim), axis, backward)  9.76 us
    another operation x3, other arithmetic  9.41 us
    ppermute x4, starting transfers between devices, padded_2(): lax.ppermute(lax.slice_in_dim(block, block.shape[dim] - width, None, axis...  9.24 us
    unnamed x4, other arithmetic  9.14 us
  transfers between devices with their start and end apart: 11, of which 7 were waited for; matrix products, arithmetic and copies ran while one was open for 25% of the time, Pallas kernels for 0%

commit v1 on v0

--- a/solution.py
+++ b/solution.py
@@ -70,7 +70,12 @@
 
 
 def local(amp_traces, patch_owner, patch_fault, patch_trace, patch_offset):
-    bricked = lax.all_to_all(amp_traces, "brick", split_axis=0, concat_axis=1, tiled=True)
+    bricked = jnp.concatenate(
+        lax.all_to_all(
+            jnp.stack(jnp.split(amp_traces, lax.axis_size("brick"), axis=0)), "brick", 0, 0
+        ),
+        axis=1,
+    )
     near_amp = padded_2(bricked, (("brick", 0), ("bulk", 1)), 1)
     energy = gradient_energy(near_amp)
     rimmed = padded_2(energy, (("brick", 1), ("bulk", 2)), 2)

time: 232 us -> 245 us (1.056)
  local copies, waits for them, and re-layouts: 20.1 us -> 32.6 us
    unnamed x15 -> x22, local copies, waits for them, and re-layouts: 8.66 us -> 19.6 us
  transfers between devices with their start and end apart: 11 -> 11, of which waited for: 7 -> 7; matrix products, arithmetic and copies ran while one was open for 25% -> 24% of each run, Pallas kernels for 0% -> 0%
where the time goes in v1:
time: 245 us; the launch traced here: 244 us
  waiting for transfers between devices  118 us (48%)
  starting transfers between devices  50.5 us (21%)
  other arithmetic  37.7 us (15%)
  local copies, waits for them, and re-layouts  32.6 us (13%)
  matrix products  4.29 us (2%)
    all_to_all x1, waiting for transfers between devices, local(): lax.all_to_all(buffer, 'bulk', split_axis=0, concat_axis=0, tiled=True)  96.4 us
    unnamed x22, local copies, waits for them, and re-layouts  19.6 us
    ppermute x4, waiting for transfers between devices, padded_2(): lax.ppermute(lax.slice_in_dim(block, 0, width, axis=dim), axis, backward)  15.8 us
    all_to_all x1, starting transfers between devices, local(): lax.all_to_all(buffer, 'bulk', split_axis=0, concat_axis=0, tiled=True)  14.7 us
    all_to_all x1, starting transfers between devices, local(): lax.all_to_all(labels, 'bulk', split_axis=0, concat_axis=0, tiled=True)  11 us
    ppermute x4, starting transfers between devices, padded_2(): lax.ppermute(lax.slice_in_dim(block, 0, width, axis=dim), axis, backward)  9.76 us
    another operation x3, other arithmetic  9.41 us
    ppermute x4, starting transfers between devices, padded_2(): lax.ppermute(lax.slice_in_dim(block, block.shape[dim] - width, None, axis...  9.24 us
  transfers between devices with their start and end apart: 11, of which 7 were waited for; matrix products, arithmetic and copies ran while one was open for 24% of the time, Pallas kernels for 0%

profile of v1, /device:TPU:24, one launch (start us, length us, event | category | flops | bytes accessed | tf_op | source)
XLA Modules:
  0.0 244.4 jit_solution(13007489855071283985)
XLA Ops:
  0.6 1.6 bitcast_dynamic-update-slice_fusion.7
  2.2 1.6 bitcast_dynamic-update-slice_fusion.6
  3.8 1.6 bitcast_dynamic-update-slice_fusion.5
  5.3 1.6 bitcast_dynamic-update-slice_fusion.4
  6.9 1.6 bitcast_dynamic-update-slice_fusion.3
  8.5 1.6 bitcast_dynamic-update-slice_fusion.2
  10.0 1.6 bitcast_dynamic-update-slice_fusion.1
  11.6 1.6 bitcast_dynamic-update-slice_fusion
  13.2 5.8 %all-to-all-start = ((f32[8,16,8,256]{3,2,1,0:T(8,128)}), f32[8,16,8,256]{3,2,1,0:T(8,128)S(1)}, u32[]{:S(2)}, u32[]{:S(2)}) async-start(f32[8,16,8,256]{3,2,1,0:T(8,128)} %bitcast_dynamic-update-slice_fusion), calls=%async_computation | async-start | bytes 2097152 | tf_op jit(solution)/shard_map/all_to_all | solution.py:74
  19.0 9.1 %reduce-window.6 = s32[32,16,128]{2,1,0:T(8,128)S(1)} reduce-window(s32[32,16,128]{2,1,0:T(8,128)S(1)} %fusion.51, s32[]{:T(128)} %constant.22.clone.1), window={size=1x1x128 pad=0_0x0_0x127_0}, to_apply=%region_0.1 | reduce-window | flops 8323072 | bytes 524292 | tf_op jit(solution)/shard_map/reduce-window
  28.1 0.1 slice.326
  28.2 0.2 copy.14
  28.4 0.2 reduce-window.9
  28.6 0.1 broadcast_add_fusion
  28.8 0.1 fusion.48
  29.0 0.1 multiply_reduce_fusion
  29.1 0.1 and_reduce_fusion
  29.2 8.6 %scatter_custom_fusion = f32[8192]{0:T(1024)} fusion(s32[2048]{0:T(1024)S(1)} %broadcast_select_fusion, f32[2048]{0:T(1024)S(1)} %convert_add_fusion, f32[]{:T(128)} %constant.18.clone.1), kind=kCustom, calls=%fused_computation.146 | custom fusion | bytes 32772
  37.8 11.0 %all-to-all-start.1 = ((f32[32,1,256]{2,1,0:T(1,128)}), f32[32,1,256]{2,1,0:T(1,128)S(1)}, u32[]{:S(2)}, u32[]{:S(2)}) async-start(f32[32,1,256]{2,1,0:T(1,128)} %bitcast.24), calls=%async_computation.1 | async-start | bytes 65536 | tf_op jit(solution)/shard_map/all_to_all | solution.py:105
  48.9 2.8 %collective-permute-start = (f32[1,64,256]{2,1,0:T(8,128)S(1)}, f32[1,64,256]{2,1,0:T(8,128)S(1)}, u32[]{:S(2)}, u32[]{:S(2)}) collective-permute-start(f32[1,64,256]{2,1,0:T(8,128)S(1)} %get-tuple-element.13), channel_id=1, source_target_pairs={{0,32},{32,64},{64,96},{96,128},{128,160},{160,192},{192,224},{1,3... | collective-permute-start | bytes 196616 | tf_op jit(solution)/shard_map/ppermute | solution.py:15
  51.7 3.1 %collective-permute-start.1 = (f32[1,64,256]{2,1,0:T(8,128)S(1)}, f32[1,64,256]{2,1,0:T(8,128)S(1)}, u32[]{:S(2)}, u32[]{:S(2)}) collective-permute-start(f32[1,64,256]{2,1,0:T(8,128)S(1)} %get-tuple-element.14), channel_id=1, source_target_pairs={{32,0},{64,32},{96,64},{128,96},{160,128},{192,160},{224,192},{33,... | collective-permute-start | bytes 196616 | tf_op jit(solution)/shard_map/ppermute | solution.py:18
  54.8 0.1 copy_bitcast_fusion
  54.9 0.2 collective-permute-done
  55.1 4.9 %collective-permute-done.1 = f32[1,64,256]{2,1,0:T(8,128)S(1)} collective-permute-done((f32[1,64,256]{2,1,0:T(8,128)S(1)}, f32[1,64,256]{2,1,0:T(8,128)S(1)}, u32[]{:S(2)}, u32[]{:S(2)}) %collective-permute-start.1) | collective-permute-done | bytes 65568 | tf_op jit(solution)/shard_map/ppermute | solution.py:18
  60.0 1.3 collective-permute-start.2
  61.3 1.3 collective-permute-start.3
  62.6 3.8 %collective-permute-done.3 = f32[18,1,256]{2,1,0:T(1,128)S(1)} collective-permute-done((f32[18,1,256]{2,1,0:T(1,128)S(1)}, f32[18,1,256]{2,1,0:T(1,128)S(1)}, u32[]{:S(2)}, u32[]{:S(2)}) %collective-permute-start.3) | collective-permute-done | bytes 18464 | tf_op jit(solution)/shard_map/ppermute | solution.py:18
  66.4 0.9 fusion.42
  67.4 1.9 collective-permute-start.4
  69.3 3.9 %collective-permute-start.5 = (f32[3,2,64,256]{3,2,1,0:T(8,128)S(1)}, f32[3,2,64,256]{3,2,1,0:T(8,128)S(1)}, u32[]{:S(2)}, u32[]{:S(2)}) collective-permute-start(f32[3,2,64,256]{3,2,1,0:T(8,128)S(1)} %get-tuple-element.5), channel_id=1, source_target_pairs={{32,0},{64,32},{96,64},{128,96},{160,128},{192,160},{224,192},{33,... | collective-permute-start | bytes 1179656 | tf_op jit(solution)/shard_map/ppermute | solution.py:18
  73.2 0.2 pad_maximum_fusion.1
  73.4 0.2 slice_add_fusion.8
  73.6 0.2 fusion.43
  73.9 5.9 %collective-permute-done.4 = f32[3,2,64,256]{3,2,1,0:T(8,128)S(1)} collective-permute-done((f32[3,2,64,256]{3,2,1,0:T(8,128)S(1)}, f32[3,2,64,256]{3,2,1,0:T(8,128)S(1)}, u32[]{:S(2)}, u32[]{:S(2)}) %collective-permute-start.4) | collective-permute-done | bytes 393248 | tf_op jit(solution)/shard_map/ppermute | solution.py:15
  79.7 4.0 %collective-permute-done.5 = f32[3,2,64,256]{3,2,1,0:T(8,128)S(1)} collective-permute-done((f32[3,2,64,256]{3,2,1,0:T(8,128)S(1)}, f32[3,2,64,256]{3,2,1,0:T(8,128)S(1)}, u32[]{:S(2)}, u32[]{:S(2)}) %collective-permute-start.5) | collective-permute-done | bytes 393248 | tf_op jit(solution)/shard_map/ppermute | solution.py:18
  83.8 3.3 %collective-permute-start.6 = (f32[3,20,2,256]{3,2,1,0:T(2,128)S(1)}, f32[3,20,2,256]{3,2,1,0:T(2,128)S(1)}, u32[]{:S(2)}, u32[]{:S(2)}) collective-permute-start(f32[3,20,2,256]{3,2,1,0:T(2,128)S(1)} %get-tuple-element.2), channel_id=1, source_target_pairs={{0,1},{1,2},{2,3},{3,4},{4,5},{5,6},{6,7},{7,8},{8,9},{9,10},{10,1... | collective-permute-start | bytes 368648 | tf_op jit(solution)/shard_map/ppermute | solution.py:15
  87.1 1.5 collective-permute-start.7
  88.6 0.2 slice_add_fusion.13
  88.8 3.1 %collective-permute-done.7 = f32[3,20,2,256]{3,2,1,0:T(2,128)S(1)} collective-permute-done((f32[3,20,2,256]{3,2,1,0:T(2,128)S(1)}, f32[3,20,2,256]{3,2,1,0:T(2,128)S(1)}, u32[]{:S(2)}, u32[]{:S(2)}) %collective-permute-start.7) | collective-permute-done | bytes 122912 | tf_op jit(solution)/shard_map/ppermute | solution.py:18
  92.0 0.9 pad_maximum_fusion
  92.9 0.5 slice_add_fusion
  93.3 1.2 slice_add_fusion.4
  94.6 4.9 %fusion.3 = f32[3,16,64,256]{3,2,1,0:T(8,128)} fusion(f32[3,16,64,256]{3,2,1,0:T(8,128)S(1)} %slice_add_fusion.4), kind=kLoop, calls=%fused_computation.15 | loop fusion | flops 3145728 | bytes 6291456 | tf_op jit(solution)/shard_map/add | solution.py:27
  99.5 5.9 %fusion.33 = f32[16,64,256]{2,1,0:T(8,128)S(1)} fusion(f32[3,16,64,256]{3,2,1,0:T(8,128)} %fusion.3, f32[16,64,256]{2,1,0:T(8,128)S(1)} %slice_add_fusion.13, f32[16,64,256]{2,1,0:T(8,128)S(1)} %fusion.43), kind=kLoop, calls=%fused_computation.82 | loop fusion | flops 6553600 | bytes 6291456 | tf_op jit(solution)/shard_map/mul | solution.py:55
  105.4 6.6 %gather_fusion = f32[2048,256]{1,0:T(8,128)S(1)} fusion(f32[1024,256]{1,0:T(8,128)S(1)} %bitcast.71, s32[2048]{0:T(1024)S(1)} %fusion.54), kind=kCustom, calls=%fused_computation | custom fusion | bytes 4202496 | tf_op jit(solution)/shard_map/gather | solution.py:84
  112.1 0.6 slice.328
  112.7 0.5 pad_select_fusion.6
  113.2 0.6 slice.329
  113.8 0.4 pad_select_fusion.5
  114.2 0.6 slice.330
  114.8 0.4 pad_select_fusion.4
  115.3 0.6 slice.331
  115.9 0.4 pad_select_fusion.3
  116.4 0.6 slice.332
  117.0 0.7 pad_select_fusion.2
  117.6 0.6 slice.333
  118.2 0.4 pad_select_fusion.1
  118.7 0.6 slice.334
  119.3 0.4 pad_select_fusion
  119.8 8.9 %scatter_custom_fusion.1 = f32[8192,128]{1,0:T(8,128)} fusion(s32[2048]{0:T(1024)S(1)} %broadcast_select_fusion, f32[]{:T(128)} %constant.18.clone.1, f32[2048,256]{1,0:T(8,128)S(1)} %pad_select_fusion, f32[2048,128]{1,0:T(8,128)S(1)} %slice.335, pred[2048]{0:T(1024)(128)(4,1)S(1)} %get-tuple-element.15), kind=kCustom, calls=%fused_computation.36 | custom fusion | flops 262144 | bytes 6294528
  128.8 14.7 %all-to-all-start.2 = ((f32[32,256,128]{2,1,0:T(8,128)}), f32[32,256,128]{2,1,0:T(8,128)}, u32[]{:S(2)}, u32[]{:S(2)}) async-start(f32[32,256,128]{2,1,0:T(8,128)} %bitcast.72), calls=%async_computation.2 | async-start | bytes 8388608 | tf_op jit(solution)/shard_map/all_to_all | solution.py:104
  143.5 0.3 fusion.45
  143.7 96.4 %all-to-all-done.2 = f32[32,256,128]{2,1,0:T(8,128)} async-done(((f32[32,256,128]{2,1,0:T(8,128)}), f32[32,256,128]{2,1,0:T(8,128)}, u32[]{:S(2)}, u32[]{:S(2)}) %all-to-all-start.2) | async-done | bytes 4194336 | tf_op jit(solution)/shard_map/all_to_all | solution.py:104
  240.1 4.3 %convolution_divide_fusion = f32[16,128]{1,0:T(8,128)} fusion(f32[8192,128]{1,0:T(8,128)} %bitcast.28, f32[8192]{0:T(1024)S(1)} %bitcast.76, f32[16]{0:T(128)S(1)} %iota_add_fusion, f32[16]{0:T(128)S(1)} %broadcast_maximum_fusion), kind=kOutput, calls=%fused_computation.52 | convolution fusion | flops 201459712 | bytes 4235392 | tf_op jit(solution)/shard_map/dot_general | solution.py:109
  (32 shorter events, 0.4 us)
Async XLA Ops:
  0.6 18.3 %copy-start.1 = (s32[2048,1]{0,1:T(1,128)S(1)}, s32[2048,1]{0,1:T(1,128)}, u32[]{:S(2)}) copy-start(s32[2048,1]{0,1:T(1,128)} %param.6) | copy-start | bytes 24580
  13.2 15.8 %copy-start.6 = (s32[2]{0:T(128)S(1)}, s32[2]{0:T(128)}, u32[]{:S(2)}) copy-start(s32[2]{0:T(128)} %constant.79) | copy-start | bytes 28
  13.2 15.9 %copy-start.5 = (s32[2]{0:T(128)S(1)}, s32[2]{0:T(128)}, u32[]{:S(2)}) copy-start(s32[2]{0:T(128)} %constant.82) | copy-start | bytes 28
  13.2 16.0 %copy-start.3 = (s32[2048]{0:T(1024)S(1)}, s32[2048]{0:T(1024)}, u32[]{:S(2)}) copy-start(s32[2048]{0:T(1024)} %param.7) | copy-start | bytes 24580
  13.2 24.6 %copy-start.2 = (s32[2048]{0:T(1024)S(1)}, s32[2048]{0:T(1024)}, u32[]{:S(2)}) copy-start(s32[2048]{0:T(1024)} %param.9) | copy-start | bytes 24580
  13.2 24.6 %all-to-all-start = ((f32[8,16,8,256]{3,2,1,0:T(8,128)}), f32[8,16,8,256]{3,2,1,0:T(8,128)S(1)}, u32[]{:S(2)}, u32[]{:S(2)}) async-start(f32[8,16,8,256]{3,2,1,0:T(8,128)} %bitcast_dynamic-update-slice_fusion), calls=%async_computation | async-start | bytes 2097152 | tf_op jit(solution)/shard_map/all_to_all | solution.py:74
  28.8 33.8 %copy-start.4 = (s32[2048]{0:T(1024)S(1)}, s32[2048]{0:T(1024)}, u32[]{:S(2)}) copy-start(s32[2048]{0:T(1024)} %param.8) | copy-start | bytes 24580
  37.8 90.9 %all-to-all-start.1 = ((f32[32,1,256]{2,1,0:T(1,128)}), f32[32,1,256]{2,1,0:T(1,128)S(1)}, u32[]{:S(2)}, u32[]{:S(2)}) async-start(f32[32,1,256]{2,1,0:T(1,128)} %bitcast.24), calls=%async_computation.1 | async-start | bytes 65536 | tf_op jit(solution)/shard_map/all_to_all | solution.py:105
  48.9 6.2 %collective-permute-start = (f32[1,64,256]{2,1,0:T(8,128)S(1)}, f32[1,64,256]{2,1,0:T(8,128)S(1)}, u32[]{:S(2)}, u32[]{:S(2)}) collective-permute-start(f32[1,64,256]{2,1,0:T(8,128)S(1)} %get-tuple-element.13), channel_id=1, source_target_pairs={{0,32},{32,64},{64,96},{96,128},{128,160},{160,192},{192,224},{1,3... | collective-permute-start | bytes 196616 | tf_op jit(solution)/shard_map/ppermute | solution.py:15
  51.7 8.3 %collective-permute-start.1 = (f32[1,64,256]{2,1,0:T(8,128)S(1)}, f32[1,64,256]{2,1,0:T(8,128)S(1)}, u32[]{:S(2)}, u32[]{:S(2)}) collective-permute-start(f32[1,64,256]{2,1,0:T(8,128)S(1)} %get-tuple-element.14), channel_id=1, source_target_pairs={{32,0},{64,32},{96,64},{128,96},{160,128},{192,160},{224,192},{33,... | collective-permute-start | bytes 196616 | tf_op jit(solution)/shard_map/ppermute | solution.py:18
  60.0 2.6 %collective-permute-start.2 = (f32[18,1,256]{2,1,0:T(1,128)S(1)}, f32[18,1,256]{2,1,0:T(1,128)S(1)}, u32[]{:S(2)}, u32[]{:S(2)}) collective-permute-start(f32[18,1,256]{2,1,0:T(1,128)S(1)} %get-tuple-element.11), channel_id=1, source_target_pairs={{0,1},{1,2},{2,3},{3,4},{4,5},{5,6},{6,7},{7,8},{8,9},{9,10},{10,1... | collective-permute-start | bytes 55304 | tf_op jit(solution)/shard_map/ppermute | solution.py:15
  61.3 5.1 %collective-permute-start.3 = (f32[18,1,256]{2,1,0:T(1,128)S(1)}, f32[18,1,256]{2,1,0:T(1,128)S(1)}, u32[]{:S(2)}, u32[]{:S(2)}) collective-permute-start(f32[18,1,256]{2,1,0:T(1,128)S(1)} %get-tuple-element.10), channel_id=1, source_target_pairs={{1,0},{2,1},{3,2},{4,3},{5,4},{6,5},{7,6},{8,7},{9,8},{10,9},{11,1... | collective-permute-start | bytes 55304 | tf_op jit(solution)/shard_map/ppermute | solution.py:18
  67.4 12.4 %collective-permute-start.4 = (f32[3,2,64,256]{3,2,1,0:T(8,128)S(1)}, f32[3,2,64,256]{3,2,1,0:T(8,128)S(1)}, u32[]{:S(2)}, u32[]{:S(2)}) collective-permute-start(f32[3,2,64,256]{3,2,1,0:T(8,128)S(1)} %get-tuple-element.4), channel_id=1, source_target_pairs={{0,32},{32,64},{64,96},{96,128},{128,160},{160,192},{192,224},{1,3... | collective-permute-start | bytes 1179656 | tf_op jit(solution)/shard_map/ppermute | solution.py:15
  69.3 14.5 %collective-permute-start.5 = (f32[3,2,64,256]{3,2,1,0:T(8,128)S(1)}, f32[3,2,64,256]{3,2,1,0:T(8,128)S(1)}, u32[]{:S(2)}, u32[]{:S(2)}) collective-permute-start(f32[3,2,64,256]{3,2,1,0:T(8,128)S(1)} %get-tuple-element.5), channel_id=1, source_target_pairs={{32,0},{64,32},{96,64},{128,96},{160,128},{192,160},{224,192},{33,... | collective-permute-start | bytes 1179656 | tf_op jit(solution)/shard_map/ppermute | solution.py:18
  83.8 5.0 %collective-permute-start.6 = (f32[3,20,2,256]{3,2,1,0:T(2,128)S(1)}, f32[3,20,2,256]{3,2,1,0:T(2,128)S(1)}, u32[]{:S(2)}, u32[]{:S(2)}) collective-permute-start(f32[3,20,2,256]{3,2,1,0:T(2,128)S(1)} %get-tuple-element.2), channel_id=1, source_target_pairs={{0,1},{1,2},{2,3},{3,4},{4,5},{5,6},{6,7},{7,8},{8,9},{9,10},{10,1... | collective-permute-start | bytes 368648 | tf_op jit(solution)/shard_map/ppermute | solution.py:15
  87.1 4.8 %collective-permute-start.7 = (f32[3,20,2,256]{3,2,1,0:T(2,128)S(1)}, f32[3,20,2,256]{3,2,1,0:T(2,128)S(1)}, u32[]{:S(2)}, u32[]{:S(2)}) collective-permute-start(f32[3,20,2,256]{3,2,1,0:T(2,128)S(1)} %get-tuple-element.3), channel_id=1, source_target_pairs={{1,0},{2,1},{3,2},{4,3},{5,4},{6,5},{7,6},{8,7},{9,8},{10,9},{11,1... | collective-permute-start | bytes 368648 | tf_op jit(solution)/shard_map/ppermute | solution.py:18
  105.4 6.7 %copy-start = (f32[16,64,256]{2,1,0:T(8,128)}, f32[16,64,256]{2,1,0:T(8,128)S(1)}, u32[]{:S(2)}) copy-start(f32[16,64,256]{2,1,0:T(8,128)S(1)} %fusion.33) | copy-start | bytes 3145732
  128.8 111.4 %all-to-all-start.2 = ((f32[32,256,128]{2,1,0:T(8,128)}), f32[32,256,128]{2,1,0:T(8,128)}, u32[]{:S(2)}, u32[]{:S(2)}) async-start(f32[32,256,128]{2,1,0:T(8,128)} %bitcast.72), calls=%async_computation.2 | async-start | bytes 8388608 | tf_op jit(solution)/shard_map/all_to_all | solution.py:104
